TPU v7x, 32 devices: a whole 2x2x4 slice. The times are simulated.
32 devices in a mesh: groups: 2 (over x), ctx: 16 (over z, y, core).
Axes of the slice: x: 2, y: 2, z: 4, core: 2. Of those that a mesh axis runs over, the one named last changes fastest.
Arguments:
- query_input: bfloat16 [32, 1536], P('groups'), parts along dimension 0, may hold values from -20 to 20
- query_gain: bfloat16 [1536], replicated, may hold values from 0.5 to 1.5
- nope_weight: bfloat16 [1536, 4096], P(None, 'ctx'), may hold values from -0.15625 to 0.15625
- rope_weight: bfloat16 [1536, 2048], P(None, 'ctx'), may hold values from -0.15625 to 0.15625
- key_up: bfloat16 [32, 128, 512], P('ctx'), may hold values from -0.5 to 0.5
- value_up: bfloat16 [32, 512, 128], P('ctx'), may hold values from -1 to 1
- out_weight: bfloat16 [4096, 7168], P('ctx'), may hold values from -0.09375 to 0.09375
- cache_latent: bfloat16 [4, 32768, 512], P('groups', 'ctx'), parts along dimension 0, may hold values from -8 to 8
- cache_rope: bfloat16 [4, 64, 32768], P('groups', None, 'ctx'), parts along dimension 0, may hold values from -256 to 256
- cached_length: int32 [4], P('groups'), parts along dimension 0, may hold values from 16384 to 32760, as said below
Outputs:
- attn_out: bfloat16 [32, 7168], P('groups'), parts along dimension 0
There are 2 independent parts, one for each index of `groups`. A program takes and returns all parts, laid end to end along the dimension named above; an argument that names none is the same for every part. Nothing has to cross between parts.
Inputs may be any that keep to these rules, and one draw needn't show every extreme that they name: `cached_length`: in every part one request has exactly 32760, so that its last new token sees the cache's last position.
All inputs are finite; a program needn't handle non-finite values.
Results may differ from a plain program's by a relative error of at most 0.012.
Values may be sent and summed in bfloat16 or wider, within the bound.
A program may use at most 128 MiB of HBM per device.

v0:
```python
import math
import jax
import jax.numpy as jnp
from jax import lax
from jax.sharding import PartitionSpec as P

mscale_yarn = 1.0 + 0.1 * math.log(40.0)
masked_score = -1e30


def attend_heads(
    latent_query, rope_query, cache_latent, cache_rope, cached_length, positions, softmax_scale
):
    row_count, head_count, latent_width = latent_query.shape
    rope_width = rope_query.shape[2]
    requests = cache_latent.shape[0]
    stretch_rows = row_count // requests
    peak_list, sum_list, pool_list = ([], [], [])
    for request in range(requests):
        flat_latent = latent_query[request * stretch_rows : (request + 1) * stretch_rows].reshape(
            stretch_rows * head_count, latent_width
        )
        flat_rope = rope_query[request * stretch_rows : (request + 1) * stretch_rows].reshape(
            stretch_rows * head_count, rope_width
        )
        scores = jnp.einsum(
            "ql,pl->qp", flat_latent, cache_latent[request], preferred_element_type=jnp.float32
        )
        scores = (
            scores + jnp.dot(flat_rope, cache_rope[request], preferred_element_type=jnp.float32)
        ) * softmax_scale
        last_seen = (
            cached_length[request]
            + jnp.arange(stretch_rows * head_count, dtype=jnp.int32) // head_count
        )
        visible = positions[None, :] <= last_seen[:, None]
        scores = jnp.where(visible, scores, masked_score)
        block_peak = jnp.max(scores, axis=1)
        weights = jnp.where(visible, jnp.exp(scores - block_peak[:, None]), 0.0)
        block_sum = jnp.sum(weights, axis=1)
        block_pool = jnp.dot(
            weights.astype(jnp.bfloat16), cache_latent[request], preferred_element_type=jnp.float32
        )
        peak_list.append(block_peak.reshape(stretch_rows, head_count))
        sum_list.append(block_sum.reshape(stretch_rows, head_count))
        pool_list.append(block_pool.reshape(stretch_rows, head_count, latent_width))
    return (
        jnp.concatenate(peak_list, axis=0),
        jnp.concatenate(sum_list, axis=0),
        jnp.concatenate(pool_list, axis=0),
    )


def project_heads(pooled, weight_sum, value_up, out_weight):
    attended = (pooled / weight_sum[:, :, None]).astype(jnp.bfloat16)
    head_values = jnp.einsum(
        "rhl,hlv->rhv", attended, value_up, preferred_element_type=jnp.float32
    ).astype(jnp.bfloat16)
    return jnp.dot(
        head_values.reshape(head_values.shape[0], -1),
        out_weight,
        preferred_element_type=jnp.float32,
    )


def local(
    query_input,
    query_gain,
    nope_weight,
    rope_weight,
    key_up,
    value_up,
    out_weight,
    cache_latent,
    cache_rope,
    cached_length,
):
    head_local = key_up.shape[0]
    nope_width = key_up.shape[1]
    rope_width = rope_weight.shape[1] // head_local
    row_count = query_input.shape[0]
    key_count = cache_latent.shape[1]
    widened = query_input.astype(jnp.float32)
    normed = (
        widened
        * lax.rsqrt(jnp.mean(widened * widened, axis=-1, keepdims=True) + 1e-06)
        * query_gain.astype(jnp.float32)
    ).astype(jnp.bfloat16)
    query_nope = (
        jnp.dot(normed, nope_weight, preferred_element_type=jnp.float32)
        .astype(jnp.bfloat16)
        .reshape(row_count, head_local, nope_width)
    )
    query_rope = (
        jnp.dot(normed, rope_weight, preferred_element_type=jnp.float32)
        .astype(jnp.bfloat16)
        .reshape(row_count, head_local, rope_width)
    )
    query_latent = jnp.einsum(
        "rhn,hnl->rhl", query_nope, key_up, preferred_element_type=jnp.float32
    ).astype(jnp.bfloat16)
    softmax_scale = mscale_yarn * mscale_yarn / math.sqrt(nope_width + rope_width)
    positions = lax.axis_index("ctx") * key_count + jnp.arange(key_count, dtype=jnp.int32)
    every_latent, every_rope = (
        lax.all_gather(query_latent, "ctx", axis=1, tiled=True),
        lax.all_gather(query_rope, "ctx", axis=1, tiled=True),
    )
    block_peak, block_sum, block_pool = attend_heads(
        every_latent, every_rope, cache_latent, cache_rope, cached_length, positions, softmax_scale
    )
    pooled_in = lax.all_to_all(block_pool[None], "ctx", split_axis=2, concat_axis=0, tiled=True)
    peak_in = lax.all_to_all(block_peak[None], "ctx", split_axis=2, concat_axis=0, tiled=True)
    sum_in = lax.all_to_all(block_sum[None], "ctx", split_axis=2, concat_axis=0, tiled=True)
    row_top = jnp.max(peak_in, axis=0)
    factor = jnp.exp(peak_in - row_top[None])
    pooled = jnp.sum(pooled_in * factor[..., None], axis=0)
    weight_sum = jnp.sum(sum_in * factor, axis=0)
    partial_value = project_heads(pooled, weight_sum, value_up, out_weight)
    return lax.psum(partial_value, "ctx").astype(jnp.bfloat16)


def solution(mesh):
    placed = (
        P("groups", None),
        P(),
        P(None, "ctx"),
        P(None, "ctx"),
        P("ctx", None, None),
        P("ctx", None, None),
        P("ctx", None),
        P("groups", "ctx", None),
        P("groups", None, "ctx"),
        P("groups"),
    )
    return jax.shard_map(
        local, mesh=mesh, in_specs=placed, out_specs=P("groups", None), check_vma=False
    )
```

profile of v0, /device:TPU:0, one launch (start us, length us, event | category | flops | bytes accessed | tf_op | source)
XLA Modules:
  0.0 175.1 jit_solution(12115778293265833145)
XLA Ops:
  0.0 0.0 copy-start
  0.0 0.0 copy-start.4
  0.0 0.0 copy-start.5
  0.0 1.4 fusion.44
  1.4 0.7 convert_element_type.40
  2.1 0.9 fusion.28
  3.1 0.0 copy-done
  3.1 1.1 fusion.21
  4.1 1.1 fusion.20
  5.2 24.6 %all_gather.6 = bf16[16,32,512]{2,0,1:T(8,128)(2,1)S(1)} all-gather(bf16[16,2,512]{2,0,1:T(8,128)(2,1)S(1)} %fusion.20), channel_id=1, replica_groups=mesh['groups'=2,'ctx'=16] {'ctx'}, dimensions={1}, use_global_device_ids=true | all-gather | bytes 557056 | tf_op jit(solution)/shard_map/all_gather | solution.py:105
  29.9 0.1 copy.76
  30.0 0.0 copy-done.4
  30.0 0.0 copy-done.5
  30.0 0.2 convolution_convert_fusion.3
  30.2 0.1 reshape.79
  30.3 17.8 %all_gather.7 = bf16[16,32,64]{2,0,1:T(8,128)(2,1)S(1)} all-gather(bf16[16,2,64]{2,0,1:T(8,128)(2,1)S(1)} %copy.64), channel_id=1, replica_groups=mesh['groups'=2,'ctx'=16] {'ctx'}, dimensions={1}, use_global_device_ids=true | all-gather | bytes 69632 | tf_op jit(solution)/shard_map/all_gather | solution.py:106
  48.1 0.1 copy.75
  48.2 0.0 copy-start.1
  48.2 2.5 %fusion.6 = f32[256,2048]{1,0:T(8,128)S(1)} fusion(bf16[256,512]{1,0:T(8,128)(2,1)S(1)} %bitcast.80, bf16[2,2048,512]{2,1,0:T(8,128)(2,1)} %param.17), kind=kOutput, calls=%fused_computation.10 | convolution fusion | flops 536870912 | bytes 4456448 | tf_op jit(solution)/shard_map/ql,pl->qp/dot_general | solution.py:26
  50.7 0.3 copy-done.1
  51.0 0.0 copy-start.3
  51.0 0.7 fusion.10
  51.8 1.3 broadcast_add_fusion
  53.1 0.0 copy-done.3
  53.1 0.6 fusion.46
  53.8 0.6 fusion.45
  54.4 1.0 fusion.16
  55.5 0.1 reshape.85
  55.5 0.1 reshape.86
  55.6 0.7 copy.72
  56.3 3.5 %all-to-all-start.2 = ((f32[1,16,32]{1,0,2:T(1,128)}), f32[1,16,32]{1,0,2:T(1,128)S(1)}, u32[]{:S(2)}, u32[]{:S(2)}) async-start(f32[1,16,32]{1,0,2:T(1,128)} %copy.72), calls=%async_computation.2 | async-start | bytes 32768 | tf_op jit(solution)/shard_map/all_to_all | solution.py:113
  59.8 0.1 reshape.84
  59.9 0.1 reshape.83
  60.0 0.0 copy-start.2
  60.0 2.4 %fusion.4 = f32[8,32,512]{2,1,0:T(8,128)S(1)} fusion(bf16[8,32,2048]{2,1,0:T(8,128)(2,1)S(1)} %bitcast.79, bf16[2,2048,512]{2,1,0:T(8,128)(2,1)} %param.17), kind=kOutput, calls=%fused_computation.8 | convolution fusion | flops 536870912 | bytes 3670016 | tf_op jit(solution)/shard_map/dot_general | solution.py:41
  62.4 0.4 copy-done.2
  62.8 0.7 fusion.8
  63.5 0.7 copy.70
  64.2 2.1 %all-to-all-done.2 = f32[1,16,32]{1,0,2:T(1,128)S(1)} async-done(((f32[1,16,32]{1,0,2:T(1,128)}), f32[1,16,32]{1,0,2:T(1,128)S(1)}, u32[]{:S(2)}, u32[]{:S(2)}) %all-to-all-start.2) | async-done | bytes 2080 | tf_op jit(solution)/shard_map/all_to_all | solution.py:113
  66.3 3.9 %all-to-all-start.1 = ((f32[1,16,32]{1,0,2:T(1,128)}), f32[1,16,32]{1,0,2:T(1,128)S(1)}, u32[]{:S(2)}, u32[]{:S(2)}) async-start(f32[1,16,32]{1,0,2:T(1,128)} %copy.70), calls=%async_computation.1 | async-start | bytes 32768 | tf_op jit(solution)/shard_map/all_to_all | solution.py:112
  70.2 0.1 maximum_bitcast_fusion
  70.3 1.6 copy.68
  71.9 0.0 copy-start.6
  71.9 4.8 %all-to-all-done.1 = f32[1,16,32]{1,0,2:T(1,128)S(1)} async-done(((f32[1,16,32]{1,0,2:T(1,128)}), f32[1,16,32]{1,0,2:T(1,128)S(1)}, u32[]{:S(2)}, u32[]{:S(2)}) %all-to-all-start.1) | async-done | bytes 2080 | tf_op jit(solution)/shard_map/all_to_all | solution.py:112
  76.7 3.7 %all-to-all-start = ((f32[1,16,32,512]{3,1,0,2:T(8,128)}), f32[1,16,32,512]{3,1,0,2:T(8,128)S(1)}, u32[]{:S(2)}, u32[]{:S(2)}) async-start(f32[1,16,32,512]{3,1,0,2:T(8,128)} %copy.68), calls=%async_computation | async-start | bytes 2097152 | tf_op jit(solution)/shard_map/all_to_all | solution.py:111
  80.4 0.2 copy.71
  80.6 22.6 %all-to-all-done = f32[1,16,32,512]{3,1,0,2:T(8,128)S(1)} async-done(((f32[1,16,32,512]{3,1,0,2:T(8,128)}), f32[1,16,32,512]{3,1,0,2:T(8,128)S(1)}, u32[]{:S(2)}, u32[]{:S(2)}) %all-to-all-start) | async-done | bytes 1048608 | tf_op jit(solution)/shard_map/all_to_all | solution.py:111
  103.2 1.1 fusion.23
  104.3 0.0 copy-done.6
  104.3 0.2 fusion.22
  104.5 2.6 %fusion.36 = f32[16,7168]{1,0:T(8,128)S(1)} fusion(bf16[256,7168]{1,0:T(8,128)(2,1)} %param.16, bf16[2,2,8,128]{3,2,1,0:T(8,128)(2,1)S(1)} %fusion.22), kind=kOutput, calls=%fused_computation.48 | convolution fusion | flops 58720256 | bytes 4136960 | tf_op jit(solution)/shard_map/dot_general | solution.py:59
  107.1 68.0 %all-reduce.1 = bf16[16,7168]{1,0:T(8,128)(2,1)} all-reduce(f32[16,7168]{1,0:T(8,128)S(1)} %fusion.36), channel_id=1, replica_groups=mesh['groups'=2,'ctx'=16] {'ctx'}, use_global_device_ids=true, to_apply=%region_8.9 | all-reduce | flops 114688 | bytes 688128 | tf_op jit(solution)/shard_map/psum | solution.py:119
  (11 shorter events, 0.2 us)
Async XLA Ops:
  0.0 3.1 %copy-start = (bf16[1536,256]{1,0:T(8,128)(2,1)S(1)}, bf16[1536,256]{1,0:T(8,128)(2,1)}, u32[]{:S(2)}) copy-start(bf16[1536,256]{1,0:T(8,128)(2,1)} %param.12) | copy-start | bytes 2359300
  0.0 30.0 %copy-start.4 = (bf16[16,1536]{1,0:T(8,128)(2,1)S(1)}, bf16[16,1536]{1,0:T(8,128)(2,1)}, u32[]{:S(2)}) copy-start(bf16[16,1536]{1,0:T(8,128)(2,1)} %param.10) | copy-start | bytes 147460
  0.0 30.0 %copy-start.5 = (bf16[1536,128]{1,0:T(8,128)(2,1)S(1)}, bf16[1536,128]{1,0:T(8,128)(2,1)}, u32[]{:S(2)}) copy-start(bf16[1536,128]{1,0:T(8,128)(2,1)} %param.13) | copy-start | bytes 1179652
  48.2 2.8 %copy-start.1 = (bf16[2,2048,512]{2,1,0:T(8,128)(2,1)S(1)}, bf16[2,2048,512]{2,1,0:T(8,128)(2,1)}, u32[]{:S(2)}) copy-start(bf16[2,2048,512]{2,1,0:T(8,128)(2,1)} %param.17) | copy-start | bytes 12582916
  51.0 2.1 %copy-start.3 = (bf16[2,64,2048]{2,1,0:T(8,128)(2,1)S(1)}, bf16[2,64,2048]{2,1,0:T(8,128)(2,1)}, u32[]{:S(2)}) copy-start(bf16[2,64,2048]{2,1,0:T(8,128)(2,1)} %param.18) | copy-start | bytes 1572868
  56.3 10.0 %all-to-all-start.2 = ((f32[1,16,32]{1,0,2:T(1,128)}), f32[1,16,32]{1,0,2:T(1,128)S(1)}, u32[]{:S(2)}, u32[]{:S(2)}) async-start(f32[1,16,32]{1,0,2:T(1,128)} %copy.72), calls=%async_computation.2 | async-start | bytes 32768 | tf_op jit(solution)/shard_map/all_to_all | solution.py:113
  60.0 2.8 %copy-start.2 = (bf16[2,2048,512]{2,1,0:T(8,128)(2,1)S(1)}, bf16[2,2048,512]{2,1,0:T(8,128)(2,1)}, u32[]{:S(2)}) copy-start(bf16[2,2048,512]{2,1,0:T(8,128)(2,1)} %param.17) | copy-start | bytes 12582916
  66.3 10.4 %all-to-all-start.1 = ((f32[1,16,32]{1,0,2:T(1,128)}), f32[1,16,32]{1,0,2:T(1,128)S(1)}, u32[]{:S(2)}, u32[]{:S(2)}) async-start(f32[1,16,32]{1,0,2:T(1,128)} %copy.70), calls=%async_computation.1 | async-start | bytes 32768 | tf_op jit(solution)/shard_map/all_to_all | solution.py:112
  71.9 32.4 %copy-start.6 = (bf16[2,512,128]{2,1,0:T(8,128)(2,1)S(1)}, bf16[2,512,128]{2,1,0:T(8,128)(2,1)}, u32[]{:S(2)}) copy-start(bf16[2,512,128]{2,1,0:T(8,128)(2,1)} %param.15) | copy-start | bytes 786436
  76.7 26.5 %all-to-all-start = ((f32[1,16,32,512]{3,1,0,2:T(8,128)}), f32[1,16,32,512]{3,1,0,2:T(8,128)S(1)}, u32[]{:S(2)}, u32[]{:S(2)}) async-start(f32[1,16,32,512]{3,1,0,2:T(8,128)} %copy.68), calls=%async_computation | async-start | bytes 2097152 | tf_op jit(solution)/shard_map/all_to_all | solution.py:111
where the time goes:
time: 176 us; the launch traced here: 175 us
  blocking collectives  110 us (62%)
  waiting for transfers between devices  29.5 us (17%)
  matrix products  12.8 us (7%)
  starting transfers between devices  11 us (6%)
  local copies, waits for them, and re-layouts  5.92 us (3%)
  other arithmetic  5.27 us (3%)
    psum x1, blocking collectives, local(): return lax.psum(partial_value, 'ctx').astype(jnp.bfloat16)  68 us
    all_gather x1, blocking collectives, local(): lax.all_gather(query_latent, 'ctx', axis=1, tiled=True)  24.6 us
    all_to_all x1, waiting for transfers between devices, local(): lax.all_to_all(block_pool[None], 'ctx', split_axis=2, concat_axis=0, tile...  22.6 us
    all_gather x1, blocking collectives, local(): lax.all_gather(query_rope, 'ctx', axis=1, tiled=True)  17.8 us
    all_to_all x1, waiting for transfers between devices, local(): lax.all_to_all(block_peak[None], 'ctx', split_axis=2, concat_axis=0, tile...  4.8 us
    all_to_all x1, starting transfers between devices, local(): lax.all_to_all(block_peak[None], 'ctx', split_axis=2, concat_axis=0, tile...  3.88 us
    all_to_all x1, starting transfers between devices, local(): lax.all_to_all(block_pool[None], 'ctx', split_axis=2, concat_axis=0, tile...  3.65 us
  transfers between devices with their start and end apart: 3, of which 3 were waited for; matrix products, arithmetic and copies ran while one was open for 3% of the time, Pallas kernels for 0%

commit v1 on v0

--- a/solution.py
+++ b/solution.py
@@ -116,7 +116,7 @@
     pooled = jnp.sum(pooled_in * factor[..., None], axis=0)
     weight_sum = jnp.sum(sum_in * factor, axis=0)
     partial_value = project_heads(pooled, weight_sum, value_up, out_weight)
-    return lax.psum(partial_value, "ctx").astype(jnp.bfloat16)
+    return jnp.sum(lax.all_gather(partial_value, "ctx"), axis=0).astype(jnp.bfloat16)
 
 
 def solution(mesh):

time: 176 us -> 203 us (1.15)
  waiting for transfers between devices: 29.5 us -> 97.3 us
  blocking collectives: 110 us -> 42.3 us
  between operations: 0.19 us -> 13.6 us
  other arithmetic: 5.27 us -> 12.3 us
  matrix products: 12.8 us -> 18.1 us
  starting transfers between devices: 11 us -> 13.1 us
    all_gather x0 -> x1, waiting for transfers between devices: none -> 69.9 us  [local(): lax.all_gather(partial_value, 'ctx')]
    psum x1 -> x0, blocking collectives: 68 us -> none  [local(): return lax.psum(partial_value, 'ctx').astype(jnp.bfloat16)]
    all_gather x1, blocking collectives: 24.6 us -> 18.9 us  [local(): lax.all_gather(query_latent, 'ctx', axis=1, tiled=True)]
    all_gather x1, blocking collectives: 17.8 us -> 23.5 us  [local(): lax.all_gather(query_rope, 'ctx', axis=1, tiled=True)]
    all_to_all x1, waiting for transfers between devices: 4.8 us -> 0.01 us  [local(): lax.all_to_all(block_peak[None], 'ctx', split_axis=2, concat_axis=0, tile...]
    reduce_sum x0 -> x1, other arithmetic: none -> 4.17 us  [local(): jnp.sum(lax.all_gather(partial_value, 'ctx'), axis=0).astype(jnp.bfloat16)]
    reduce_sum x1, other arithmetic: 1.04 us -> 3.83 us  [attend_heads(): block_sum = jnp.sum(weights, axis=1)]
    all_to_all x1, waiting for transfers between devices: 2.1 us -> 4.8 us  [local(): lax.all_to_all(block_sum[None], 'ctx', split_axis=2, concat_axis=0, tiled...]
  transfers between devices with their start and end apart: 3 -> 4, of which waited for: 3 -> 3; matrix products, arithmetic and copies ran while one was open for 3% -> 6% of each run, Pallas kernels for 0% -> 0%
where the time goes in v1:
time: 203 us; the launch traced here: 202 us
  waiting for transfers between devices  97.3 us (48%)
  blocking collectives  42.3 us (21%)
  matrix products  18.1 us (9%)
  between operations  13.6 us (7%)
  starting transfers between devices  13.1 us (6%)
  other arithmetic  12.3 us (6%)
  local copies, waits for them, and re-layouts  5.56 us (3%)
    all_gather x1, waiting for transfers between devices, local(): lax.all_gather(partial_value, 'ctx')  69.9 us
    all_gather x1, blocking collectives, local(): lax.all_gather(query_rope, 'ctx', axis=1, tiled=True)  23.5 us
    all_to_all x1, waiting for transfers between devices, local(): lax.all_to_all(block_pool[None], 'ctx', split_axis=2, concat_axis=0, tile...  22.6 us
    all_gather x1, blocking collectives, local(): lax.all_gather(query_latent, 'ctx', axis=1, tiled=True)  18.9 us
    all_to_all x1, starting transfers between devices, local(): lax.all_to_all(block_sum[None], 'ctx', split_axis=2, concat_axis=0, tiled...  5.97 us
    all_to_all x1, waiting for transfers between devices, local(): lax.all_to_all(block_sum[None], 'ctx', split_axis=2, concat_axis=0, tiled...  4.8 us
    dot_general x2, matrix products, attend_heads(): jnp.einsum('ql,pl->qp', flat_latent, cache_latent[request], preferred_ele...  4.8 us
    dot_general x2, matrix products, attend_heads(): jnp.dot(weights.astype(jnp.bfloat16), cache_latent[request], preferred_el...  4.68 us
  transfers between devices with their start and end apart: 4, of which 3 were waited for; matrix products, arithmetic and copies ran while one was open for 6% of the time, Pallas kernels for 0%

profile of v1, /device:TPU:0, one launch (start us, length us, event | category | flops | bytes accessed | tf_op | source)
XLA Modules:
  0.0 202.3 jit_solution(3345271216129224351)
XLA Ops:
  6.5 0.0 copy-start
  6.5 0.0 copy-start.4
  6.5 1.0 fusion.28
  7.6 1.4 fusion.44
  9.0 0.7 convert_element_type.40
  9.7 1.2 convolution_convert_fusion.3
  10.9 0.0 copy-done
  10.9 1.1 fusion.21
  12.0 0.1 reshape.79
  12.0 23.5 %all_gather.13 = bf16[16,32,64]{2,0,1:T(8,128)(2,1)S(1)} all-gather(bf16[16,2,64]{2,0,1:T(8,128)(2,1)S(1)} %copy.64), channel_id=1, replica_groups=mesh['groups'=2,'ctx'=16] {'ctx'}, dimensions={1}, use_global_device_ids=true | all-gather | bytes 69632 | tf_op jit(solution)/shard_map/all_gather | solution.py:106
  35.6 0.0 copy-done.4
  35.6 0.1 fusion.20
  35.7 18.9 %all_gather.12 = bf16[16,32,512]{2,0,1:T(8,128)(2,1)S(1)} all-gather(bf16[16,2,512]{2,0,1:T(8,128)(2,1)S(1)} %fusion.20), channel_id=1, replica_groups=mesh['groups'=2,'ctx'=16] {'ctx'}, dimensions={1}, use_global_device_ids=true | all-gather | bytes 557056 | tf_op jit(solution)/shard_map/all_gather | solution.py:105
  54.6 0.1 copy.75
  54.7 0.1 copy.76
  54.8 1.3 broadcast_add_fusion
  56.1 0.0 copy-start.2
  56.2 2.4 %fusion.6 = f32[256,2048]{1,0:T(8,128)S(1)} fusion(bf16[256,512]{1,0:T(8,128)(2,1)S(1)} %bitcast.83, bf16[2,2048,512]{2,1,0:T(8,128)(2,1)} %param.17), kind=kOutput, calls=%fused_computation.10 | convolution fusion | flops 536870912 | bytes 4456448 | tf_op jit(solution)/shard_map/ql,pl->qp/dot_general | solution.py:26
  58.6 0.0 copy-done.2
  58.6 0.6 fusion.46
  59.2 0.1 reshape.84
  59.3 0.0 copy-start.3
  59.3 2.4 %fusion.10 = f32[256,2048]{1,0:T(8,128)S(1)} fusion(bf16[256,512]{1,0:T(8,128)(2,1)S(1)} %bitcast.82, bf16[2,2048,512]{2,1,0:T(8,128)(2,1)} %param.17), kind=kOutput, calls=%fused_computation.14 | convolution fusion | flops 536870912 | bytes 4456448 | tf_op jit(solution)/shard_map/ql,pl->qp/dot_general | solution.py:26
  61.7 0.0 copy-done.3
  61.7 1.9 fusion.45
  63.6 0.1 reshape.83
  63.7 0.7 copy.70
  64.4 3.5 %all-to-all-start.1 = ((f32[1,16,32]{1,0,2:T(1,128)}), f32[1,16,32]{1,0,2:T(1,128)S(1)}, u32[]{:S(2)}, u32[]{:S(2)}) async-start(f32[1,16,32]{1,0,2:T(1,128)} %copy.70), calls=%async_computation.1 | async-start | bytes 32768 | tf_op jit(solution)/shard_map/all_to_all | solution.py:112
  67.9 3.8 %fusion.16 = (f32[256]{0:T(256)S(1)}, f32[256]{0:T(256)S(1)}, bf16[256,2048]{1,0:T(8,128)(2,1)}, bf16[256,2048]{1,0:T(8,128)(2,1)}) fusion(f32[256,2048]{1,0:T(8,128)} %get-tuple-element.18, f32[256]{0:T(256)S(1)} %get-tuple-element.17, s32[2048]{0:T(1024)S(1)} %iota_add_fusion, s32[256]{0:T(256)S(1)} %get-tuple-element.22, ...), kind=kLoop, calls=%fused_computation.20 | loop fusion | flops 5242368 | bytes 6305792 | tf_op jit(solution)/shard_map/reduce_sum | solution.py:40
  71.7 0.1 reshape.85
  71.8 0.1 reshape.86
  71.8 0.0 copy-start.1
  71.9 2.8 %fusion.4 = f32[8,32,512]{2,1,0:T(8,128)S(1)} fusion(bf16[8,32,2048]{2,1,0:T(8,128)(2,1)} %bitcast.81, bf16[2,2048,512]{2,1,0:T(8,128)(2,1)} %param.17), kind=kOutput, calls=%fused_computation.8 | convolution fusion | flops 536870912 | bytes 3670016 | tf_op jit(solution)/shard_map/dot_general | solution.py:41
  74.6 0.4 copy-done.1
  75.0 1.9 fusion.8
  76.9 0.7 copy.72
  77.6 0.0 all-to-all-done.1
  77.6 6.0 %all-to-all-start.2 = ((f32[1,16,32]{1,0,2:T(1,128)}), f32[1,16,32]{1,0,2:T(1,128)S(1)}, u32[]{:S(2)}, u32[]{:S(2)}) async-start(f32[1,16,32]{1,0,2:T(1,128)} %copy.72), calls=%async_computation.2 | async-start | bytes 32768 | tf_op jit(solution)/shard_map/all_to_all | solution.py:113
  83.6 0.1 maximum_bitcast_fusion
  83.7 1.6 copy.68
  85.3 0.0 copy-start.5
  85.3 4.8 %all-to-all-done.2 = f32[1,16,32]{1,0,2:T(1,128)S(1)} async-done(((f32[1,16,32]{1,0,2:T(1,128)}), f32[1,16,32]{1,0,2:T(1,128)S(1)}, u32[]{:S(2)}, u32[]{:S(2)}) %all-to-all-start.2) | async-done | bytes 2080 | tf_op jit(solution)/shard_map/all_to_all | solution.py:113
  90.1 3.7 %all-to-all-start = ((f32[1,16,32,512]{3,1,0,2:T(8,128)}), f32[1,16,32,512]{3,1,0,2:T(8,128)S(1)}, u32[]{:S(2)}, u32[]{:S(2)}) async-start(f32[1,16,32,512]{3,1,0,2:T(8,128)} %copy.68), calls=%async_computation | async-start | bytes 2097152 | tf_op jit(solution)/shard_map/all_to_all | solution.py:111
  93.8 0.0 all-gather.3.cloned.1.call-start
  93.9 0.2 copy.71
  94.0 22.6 %all-to-all-done = f32[1,16,32,512]{3,1,0,2:T(8,128)S(1)} async-done(((f32[1,16,32,512]{3,1,0,2:T(8,128)}), f32[1,16,32,512]{3,1,0,2:T(8,128)S(1)}, u32[]{:S(2)}, u32[]{:S(2)}) %all-to-all-start) | async-done | bytes 1048608 | tf_op jit(solution)/shard_map/all_to_all | solution.py:111
  116.6 1.1 fusion.23
  117.7 0.0 copy-done.5
  117.7 0.2 fusion.22
  117.9 3.4 %fusion.36 = f32[16,7168]{1,0:T(8,128)} fusion(bf16[256,7168]{1,0:T(8,128)(2,1)} %param.16, bf16[2,2,8,128]{3,2,1,0:T(8,128)(2,1)S(1)} %fusion.22), kind=kOutput, calls=%fused_computation.48 | convolution fusion | flops 58720256 | bytes 4136960 | tf_op jit(solution)/shard_map/dot_general | solution.py:59
  121.3 0.0 all-gather.3.cloned.1.call-update
  121.3 69.9 %all-gather.3.cloned.1.call-done = f32[256,7168]{1,0:T(8,128)} async-done(((f32[16,7168]{1,0:T(8,128)}), f32[256,7168]{1,0:T(8,128)}) %all-gather.3.cloned.1.call-update) | async-done | bytes 7340048 | tf_op jit(solution)/shard_map/all_gather | solution.py:119
  191.3 4.2 %reduce_sum.59 = bf16[16,7168]{1,0:T(8,128)(2,1)} reduce(f32[16,16,7168]{2,1,0:T(8,128)} %bitcast.78, f32[]{:T(128)} %constant.35.clone.1), dimensions={0}, to_apply=%region_8.9 | reduce | flops 1720320 | bytes 7569412 | tf_op jit(solution)/shard_map/reduce_sum | solution.py:119
  (11 shorter events, 0.2 us)
Async XLA Ops:
  6.5 4.4 %copy-start = (bf16[1536,256]{1,0:T(8,128)(2,1)S(1)}, bf16[1536,256]{1,0:T(8,128)(2,1)}, u32[]{:S(2)}) copy-start(bf16[1536,256]{1,0:T(8,128)(2,1)} %param.12) | copy-start | bytes 2359300
  6.5 29.0 %copy-start.4 = (bf16[2,128,512]{2,1,0:T(8,128)(2,1)S(1)}, bf16[2,128,512]{2,1,0:T(8,128)(2,1)}, u32[]{:S(2)}) copy-start(bf16[2,128,512]{2,1,0:T(8,128)(2,1)} %param.14) | copy-start | bytes 786436
  56.1 2.4 %copy-start.2 = (bf16[2,64,2048]{2,1,0:T(8,128)(2,1)S(1)}, bf16[2,64,2048]{2,1,0:T(8,128)(2,1)}, u32[]{:S(2)}) copy-start(bf16[2,64,2048]{2,1,0:T(8,128)(2,1)} %param.18) | copy-start | bytes 1572868
  59.3 2.4 %copy-start.3 = (bf16[2,64,2048]{2,1,0:T(8,128)(2,1)S(1)}, bf16[2,64,2048]{2,1,0:T(8,128)(2,1)}, u32[]{:S(2)}) copy-start(bf16[2,64,2048]{2,1,0:T(8,128)(2,1)} %param.18) | copy-start | bytes 1572868
  64.4 13.2 %all-to-all-start.1 = ((f32[1,16,32]{1,0,2:T(1,128)}), f32[1,16,32]{1,0,2:T(1,128)S(1)}, u32[]{:S(2)}, u32[]{:S(2)}) async-start(f32[1,16,32]{1,0,2:T(1,128)} %copy.70), calls=%async_computation.1 | async-start | bytes 32768 | tf_op jit(solution)/shard_map/all_to_all | solution.py:112
  71.8 3.1 %copy-start.1 = (bf16[2,2048,512]{2,1,0:T(8,128)(2,1)S(1)}, bf16[2,2048,512]{2,1,0:T(8,128)(2,1)}, u32[]{:S(2)}) copy-start(bf16[2,2048,512]{2,1,0:T(8,128)(2,1)} %param.17) | copy-start | bytes 12582916
  77.6 12.5 %all-to-all-start.2 = ((f32[1,16,32]{1,0,2:T(1,128)}), f32[1,16,32]{1,0,2:T(1,128)S(1)}, u32[]{:S(2)}, u32[]{:S(2)}) async-start(f32[1,16,32]{1,0,2:T(1,128)} %copy.72), calls=%async_computation.2 | async-start | bytes 32768 | tf_op jit(solution)/shard_map/all_to_all | solution.py:113
  85.3 32.4 %copy-start.5 = (bf16[2,512,128]{2,1,0:T(8,128)(2,1)S(1)}, bf16[2,512,128]{2,1,0:T(8,128)(2,1)}, u32[]{:S(2)}) copy-start(bf16[2,512,128]{2,1,0:T(8,128)(2,1)} %param.15) | copy-start | bytes 786436
  90.1 26.5 %all-to-all-start = ((f32[1,16,32,512]{3,1,0,2:T(8,128)}), f32[1,16,32,512]{3,1,0,2:T(8,128)S(1)}, u32[]{:S(2)}, u32[]{:S(2)}) async-start(f32[1,16,32,512]{3,1,0,2:T(8,128)} %copy.68), calls=%async_computation | async-start | bytes 2097152 | tf_op jit(solution)/shard_map/all_to_all | solution.py:111
  93.8 97.5 %all-gather.3.cloned.1.call-start = ((), (), s32[]{:S(2)}) async-start(), calls=%async_computation.3 | async-start | bytes 7798784 | tf_op jit(solution)/shard_map/all_gather | solution.py:119
Sparse Core Ops, SparseCore 0:
  121.5 69.7 all-gather.2
